TPU v7x, 32 devices: a whole 2x2x4 slice. The times are simulated.
32 devices in a mesh: row: 4 (over z), col: 4 (over y, x), tm: 2 (over core).
Axes of the slice: x: 2, y: 2, z: 4, core: 2. Of those that a mesh axis runs over, the one named last changes fastest.
Arguments:
- g_occ: float32 [2, 6144, 6144], P('tm', 'row', 'col'), may hold values from -6 to 6
- g_emp: float32 [2, 6144, 6144], P('tm', 'row', 'col'), may hold values from -6 to 6
- basis: float32 [6144, 1024], P('col'), may hold values from -0.078125 to 0.078125
Outputs:
- spectrum: float32 [2, 1024, 1024], P('tm', 'row', 'col')
All inputs are finite; a program needn't handle non-finite values.
Results may differ from a plain program's by a relative error of at most 0.000071.
Values sent between devices are 32-bit elements; how exact they have to be, the bound alone decides.
No kernel may reach another device: no remote copies, remote signals or barrier semaphores. Data moves between devices by JAX's collectives and lax.ppermute only.
A program may use at most 128 MiB of HBM per device.

v0:
```python
import jax
import jax.numpy as jnp
from jax import lax
from jax.sharding import PartitionSpec as P

HIGHEST_PRECISION = lax.Precision.HIGHEST


def broadcast(block, axis, source):
    block = jnp.where(lax.axis_index(axis) == source, block, jnp.zeros_like(block))
    return lax.psum(block, axis)


def per_device(g_occ, g_emp, basis):
    response = g_occ[0] * g_emp[0]
    rows_dev = response.shape[0]
    cols_dev = basis.shape[0]
    first_row = lax.axis_index("row") * rows_dev
    owner = first_row // cols_dev
    offset_local = first_row % cols_dev
    mine = lax.dynamic_slice_in_dim(basis, offset_local, rows_dev, 0)
    panel = broadcast(mine, "col", owner)
    mixed = jnp.dot(
        response, basis, precision=HIGHEST_PRECISION, preferred_element_type=jnp.float32
    )
    mixed_rows = lax.psum_scatter(mixed, "col", scatter_dimension=1, tiled=True)
    projected = lax.psum_scatter(
        lax.dot_general(
            panel,
            mixed_rows,
            (((0,), (0,)), ((), ())),
            precision=HIGHEST_PRECISION,
            preferred_element_type=jnp.float32,
        ),
        "row",
        scatter_dimension=0,
        tiled=True,
    )
    points = lax.axis_size("tm")
    moment = lax.axis_index("tm").astype(jnp.float32)
    orders = jnp.arange(1 * lax.axis_size("tm"), dtype=jnp.int32).astype(jnp.float32)
    weights = jnp.sqrt(2.0 / points) * jnp.cos(jnp.pi * (orders + 0.5) * (moment + 0.5) / points)
    return lax.psum_scatter(
        weights[:, None, None] * projected[None, :, :], "tm", scatter_dimension=0, tiled=True
    )


def solution(mesh):
    return jax.shard_map(
        per_device,
        mesh=mesh,
        in_specs=(P("tm", "row", "col"), P("tm", "row", "col"), P("col", None)),
        out_specs=P("tm", "row", "col"),
        check_vma=False,
    )
```

profile of v0, /device:TPU:0, one launch (start us, length us, event | category | flops | bytes accessed | tf_op | source)
XLA Modules:
  0.0 283.3 jit_solution(11242491472990814980)
XLA Ops:
  6.5 0.0 all-reduce.2.cloned.1.call-start
  6.5 6.8 %broadcast_select_fusion = f32[1536,1024]{1,0:T(8,128)} fusion(f32[1536,1024]{1,0:T(8,128)} %param.5, pred[]{:T(512)S(6)} %eq.5), kind=kLoop, calls=%fused_computation.3 | loop fusion | flops 1572864 | bytes 12582913 | tf_op jit(solution)/shard_map/jit(_where)/select_n | solution.py:10
  13.4 0.0 all-reduce.2.cloned.1.call-update
  13.4 0.0 reduce-scatter.4.cloned.1.call-start
  13.4 36.6 %fusion = f32[1536,1024]{1,0:T(8,128)} fusion(f32[1536,1024]{1,0:T(8,128)} %param.5, f32[1,1536,1536]{2,1,0:T(8,128)} %param.3, f32[1,1536,1536]{2,1,0:T(8,128)} %param.4), kind=kOutput, calls=%fused_computation | convolution fusion | flops 28993388544 | bytes 31457280 | tf_op jit(solution)/shard_map/dot_general | solution.py:23
  50.1 0.0 reduce-scatter.4.cloned.1.call-update
  50.1 0.2 reduce-scatter.6.cloned.1.call-start
  50.3 104.1 %all-reduce.2.cloned.1.call-done = f32[1536,1024]{1,0:T(8,128)} async-done(((f32[1536,1024]{1,0:T(8,128)}), f32[1536,1024]{1,0:T(8,128)}) %all-reduce.2.cloned.1.call-update) | async-done | bytes 6291472 | tf_op jit(solution)/shard_map/psum | solution.py:11
  154.4 73.1 %reduce-scatter.4.cloned.1.call-done = f32[1536,256]{1,0:T(8,128)} async-done(((f32[1536,1024]{1,0:T(8,128)}), f32[1536,256]{1,0:T(8,128)}) %reduce-scatter.4.cloned.1.call-update) | async-done | bytes 1572880 | tf_op jit(solution)/shard_map/reduce_scatter | solution.py:26
  227.5 13.3 %fusion.3 = f32[1024,256]{1,0:T(8,128)} fusion(f32[1536,1024]{1,0:T(8,128)} %all-reduce.2.cloned.1.call-done, f32[1536,256]{1,0:T(8,128)} %reduce-scatter.4.cloned.1.call-done), kind=kOutput, calls=%fused_computation.6 | convolution fusion | flops 4831838208 | bytes 8912896 | tf_op jit(solution)/shard_map/dot_general | solution.py:28
  240.7 0.0 reduce-scatter.6.cloned.1.call-update
  240.8 0.0 reduce-scatter.8.cloned.1.call-start
  240.9 27.3 %reduce-scatter.6.cloned.1.call-done = f32[256,256]{1,0:T(8,128)} async-done(((f32[1024,256]{1,0:T(8,128)}), f32[256,256]{1,0:T(8,128)}) %reduce-scatter.6.cloned.1.call-update) | async-done | bytes 262160 | tf_op jit(solution)/shard_map/reduce_scatter | solution.py:27
  268.2 1.8 broadcast_multiply_fusion
  270.0 0.0 reduce-scatter.8.cloned.1.call-update
  270.1 6.7 %reduce-scatter.8.cloned.1.call-done = f32[1,256,256]{2,1,0:T(8,128)} async-done(((f32[2,256,256]{2,1,0:T(8,128)}), f32[1,256,256]{2,1,0:T(8,128)}) %reduce-scatter.8.cloned.1.call-update) | async-done | bytes 262160 | tf_op jit(solution)/shard_map/reduce_scatter | solution.py:43
  (1 shorter events, 0.0 us)
Async XLA Ops:
  6.5 147.9 %all-reduce.2.cloned.1.call-start = ((), (), s32[]{:S(2)}) async-start(), calls=%async_computation.3 | async-start | bytes 12582912 | tf_op jit(solution)/shard_map/psum | solution.py:11
  13.4 214.1 %reduce-scatter.4.cloned.1.call-start = ((), (), s32[]{:S(2)}) async-start(), calls=%async_computation.4 | async-start | bytes 7864320 | tf_op jit(solution)/shard_map/reduce_scatter | solution.py:26
  50.1 218.1 %reduce-scatter.6.cloned.1.call-start = ((), (), s32[]{:S(2)}) async-start(), calls=%async_computation.5 | async-start | bytes 1310720 | tf_op jit(solution)/shard_map/reduce_scatter | solution.py:27
  240.8 36.0 %reduce-scatter.8.cloned.1.call-start = ((), (), s32[]{:S(2)}) async-start(), calls=%async_computation.6 | async-start | bytes 786432 | tf_op jit(solution)/shard_map/reduce_scatter | solution.py:43
Sparse Core Ops, SparseCore 0:
  13.5 140.8 all-reduce.1
  157.4 70.0 reduce-scatter.3
  240.9 27.2 reduce-scatter.5
  270.3 6.4 reduce-scatter.7
where the time goes:
time: 283 us
  waiting for transfers between devices  211 us (75%)
  matrix products  49.9 us (18%)
  between operations  13.1 us (5%)
  other arithmetic  8.7 us (3%)
    psum x1, waiting for transfers between devices, broadcast(): return lax.psum(block, axis)  104 us
    reduce_scatter x1, waiting for transfers between devices, per_device(): mixed_rows = lax.psum_scatter(mixed, 'col', scatter_dimension=1, tiled=True)  73.1 us
    dot_general x1, matrix products, per_device(): jnp.dot(response, basis, precision=HIGHEST_PRECISION, preferred_element_t...  36.6 us
    reduce_scatter x1, waiting for transfers between devices, per_device(): lax.psum_scatter(lax.dot_general(panel, mixed_rows, (((0,), (0,)), ((), (...  27.3 us
    dot_general x1, matrix products, per_device(): lax.dot_general(panel, mixed_rows, (((0,), (0,)), ((), ())), precision=HI...  13.3 us
    select_n x1, other arithmetic, broadcast(): jnp.where(lax.axis_index(axis) == source, block, jnp.zeros_like(block))  6.82 us
    reduce_scatter x1, waiting for transfers between devices, per_device(): lax.psum_scatter(weights[:, None, None] * projected[None, :, :], 'tm', sc...  6.71 us
  transfers between devices with their start and end apart: 4, of which 4 were waited for; matrix products, arithmetic and copies ran while one was open for 13% of the time, Pallas kernels for 0%

commit v1 on v0

--- a/solution.py
+++ b/solution.py
@@ -8,7 +8,7 @@
 
 def broadcast(block, axis, source):
     block = jnp.where(lax.axis_index(axis) == source, block, jnp.zeros_like(block))
-    return lax.psum(block, axis)
+    return jnp.sum(lax.all_gather(block, axis), axis=0)
 
 
 def per_device(g_occ, g_emp, basis):

time: 283 us -> 373 us (1.32)
  waiting for transfers between devices: 211 us -> 288 us
  other arithmetic: 8.7 us -> 21.6 us
    all_gather x0 -> x1, waiting for transfers between devices: none -> 194 us  [broadcast(): return jnp.sum(lax.all_gather(block, axis), axis=0)]
    psum x1 -> x0, waiting for transfers between devices: 104 us -> none  [broadcast(): return lax.psum(block, axis)]
    reduce_scatter x1, waiting for transfers between devices: 73.1 us -> 60.1 us  [per_device(): mixed_rows = lax.psum_scatter(mixed, 'col', scatter_dimension=1, tiled=True)]
    reduce_sum x0 -> x1, other arithmetic: none -> 12.9 us  [broadcast(): return jnp.sum(lax.all_gather(block, axis), axis=0)]
where the time goes in v1:
time: 373 us
  waiting for transfers between devices  288 us (77%)
  matrix products  49.9 us (13%)
  other arithmetic  21.6 us (6%)
  between operations  13.1 us (4%)
    all_gather x1, waiting for transfers between devices, broadcast(): return jnp.sum(lax.all_gather(block, axis), axis=0)  194 us
    reduce_scatter x1, waiting for transfers between devices, per_device(): mixed_rows = lax.psum_scatter(mixed, 'col', scatter_dimension=1, tiled=True)  60.1 us
    dot_general x1, matrix products, per_device(): jnp.dot(response, basis, precision=HIGHEST_PRECISION, preferred_element_t...  36.6 us
    reduce_scatter x1, waiting for transfers between devices, per_device(): lax.psum_scatter(lax.dot_general(panel, mixed_rows, (((0,), (0,)), ((), (...  27.3 us
    dot_general x1, matrix products, per_device(): lax.dot_general(panel, mixed_rows, (((0,), (0,)), ((), ())), precision=HI...  13.3 us
    reduce_sum x1, other arithmetic, broadcast(): return jnp.sum(lax.all_gather(block, axis), axis=0)  12.9 us
  transfers between devices with their start and end apart: 4, of which 4 were waited for; matrix products, arithmetic and copies ran while one was open for 13% of the time, Pallas kernels for 0%

profile of v1, /device:TPU:0, one launch (start us, length us, event | category | flops | bytes accessed | tf_op | source)
XLA Modules:
  0.0 372.8 jit_solution(14354237105403860569)
XLA Ops:
  6.5 0.0 all-gather.3.cloned.1.call-start
  6.5 6.9 %broadcast_select_fusion = f32[1536,1024]{1,0:T(8,128)} fusion(f32[1536,1024]{1,0:T(8,128)} %param.5, pred[]{:T(512)S(6)} %eq.5), kind=kLoop, calls=%fused_computation.3 | loop fusion | flops 1572864 | bytes 12582913 | tf_op jit(solution)/shard_map/jit(_where)/select_n | solution.py:10
  13.4 0.0 all-gather.3.cloned.1.call-update
  13.4 0.0 reduce-scatter.4.cloned.1.call-start
  13.5 36.6 %fusion = f32[1536,1024]{1,0:T(8,128)} fusion(f32[1536,1024]{1,0:T(8,128)} %param.5, f32[1,1536,1536]{2,1,0:T(8,128)} %param.3, f32[1,1536,1536]{2,1,0:T(8,128)} %param.4), kind=kOutput, calls=%fused_computation | convolution fusion | flops 28993388544 | bytes 31457280 | tf_op jit(solution)/shard_map/dot_general | solution.py:23
  50.1 0.0 reduce-scatter.4.cloned.1.call-update
  50.1 0.2 reduce-scatter.6.cloned.1.call-start
  50.4 193.5 %all-gather.3.cloned.1.call-done = f32[6144,1024]{1,0:T(8,128)} async-done(((f32[1536,1024]{1,0:T(8,128)}), f32[6144,1024]{1,0:T(8,128)}) %all-gather.3.cloned.1.call-update) | async-done | bytes 25165840 | tf_op jit(solution)/shard_map/all_gather | solution.py:11
  243.9 12.9 %reduce_sum.9 = f32[1536,1024]{1,0:T(8,128)} reduce(f32[4,1536,1024]{2,1,0:T(8,128)} %bitcast.7, f32[]{:T(128)} %constant.37.clone.1), dimensions={0}, to_apply=%region_0.1 | reduce | flops 4718592 | bytes 31457284 | tf_op jit(solution)/shard_map/reduce_sum | solution.py:11
  256.8 60.1 %reduce-scatter.4.cloned.1.call-done = f32[1536,256]{1,0:T(8,128)} async-done(((f32[1536,1024]{1,0:T(8,128)}), f32[1536,256]{1,0:T(8,128)}) %reduce-scatter.4.cloned.1.call-update) | async-done | bytes 1572880 | tf_op jit(solution)/shard_map/reduce_scatter | solution.py:26
  316.9 13.3 %fusion.3 = f32[1024,256]{1,0:T(8,128)} fusion(f32[1536,1024]{1,0:T(8,128)} %reduce_sum.9, f32[1536,256]{1,0:T(8,128)} %reduce-scatter.4.cloned.1.call-done), kind=kOutput, calls=%fused_computation.6 | convolution fusion | flops 4831838208 | bytes 8912896 | tf_op jit(solution)/shard_map/dot_general | solution.py:28
  330.2 0.0 reduce-scatter.6.cloned.1.call-update
  330.2 0.0 reduce-scatter.8.cloned.1.call-start
  330.3 27.3 %reduce-scatter.6.cloned.1.call-done = f32[256,256]{1,0:T(8,128)} async-done(((f32[1024,256]{1,0:T(8,128)}), f32[256,256]{1,0:T(8,128)}) %reduce-scatter.6.cloned.1.call-update) | async-done | bytes 262160 | tf_op jit(solution)/shard_map/reduce_scatter | solution.py:27
  357.7 1.8 broadcast_multiply_fusion
  359.5 0.0 reduce-scatter.8.cloned.1.call-update
  359.5 6.7 %reduce-scatter.8.cloned.1.call-done = f32[1,256,256]{2,1,0:T(8,128)} async-done(((f32[2,256,256]{2,1,0:T(8,128)}), f32[1,256,256]{2,1,0:T(8,128)}) %reduce-scatter.8.cloned.1.call-update) | async-done | bytes 262160 | tf_op jit(solution)/shard_map/reduce_scatter | solution.py:43
  (1 shorter events, 0.0 us)
Async XLA Ops:
  6.5 237.3 %all-gather.3.cloned.1.call-start = ((), (), s32[]{:S(2)}) async-start(), calls=%async_computation.6 | async-start | bytes 31457280 | tf_op jit(solution)/shard_map/all_gather | solution.py:11
  13.4 303.5 %reduce-scatter.4.cloned.1.call-start = ((), (), s32[]{:S(2)}) async-start(), calls=%async_computation.3 | async-start | bytes 7864320 | tf_op jit(solution)/shard_map/reduce_scatter | solution.py:26
  50.1 307.5 %reduce-scatter.6.cloned.1.call-start = ((), (), s32[]{:S(2)}) async-start(), calls=%async_computation.4 | async-start | bytes 1310720 | tf_op jit(solution)/shard_map/reduce_scatter | solution.py:27
  330.2 36.0 %reduce-scatter.8.cloned.1.call-start = ((), (), s32[]{:S(2)}) async-start(), calls=%async_computation.5 | async-start | bytes 786432 | tf_op jit(solution)/shard_map/reduce_scatter | solution.py:43
Sparse Core Ops, SparseCore 0:
  13.5 230.2 all-gather.2
  246.9 70.0 reduce-scatter.3
  330.3 27.2 reduce-scatter.5
  359.8 6.4 reduce-scatter.7
